TPU v7x, 32 devices: a whole 2x2x4 slice. The times are simulated.
32 devices in a mesh: dp: 8 (over z, x), head: 4 (over y, core).
Axes of the slice: x: 2, y: 2, z: 4, core: 2. Of those that a mesh axis runs over, the one named last changes fastest.
Arguments:
- tokens: bfloat16 [32, 196, 216], P('dp'), may hold values from -6 to 6
- cotangent: float32 [32, 196, 216], P('dp'), may hold values from -6 to 6
- image_count: int32 [8], P('dp'), may hold values from 1 to 4, as said below
- subnet_heads: int32 [1], replicated, may hold values from 6 to 12
- subnet_width: int32 [1], replicated, may hold values from 432 to 864
- block_slot: int32 [12], replicated, may hold values from 0 to 15, as said below
- master: float32 [16, 54, 864], P('dp', None, 'head'), may hold values from -0.8164966 to 0.8164966
- master_m1: float32 [16, 54, 864], P('dp', None, 'head'), may hold values from -187.82971 to 187.82971
- master_m2: float32 [16, 54, 864], P('dp', None, 'head'), may hold values from 78 to 15680
- norm_params: float32 [4, 216], replicated, may hold values from -0.9 to 1.45
- norm_m1: float32 [4, 216], replicated, may hold values from -265.63132 to 265.63132
- norm_m2: float32 [4, 216], replicated, may hold values from 3920 to 35280
- talk: float32 [2, 12, 12], replicated, may hold values from -0.45 to 1.45
- talk_m1: float32 [2, 12, 12], replicated, may hold values from -831.55756 to 831.55756
- talk_m2: float32 [2, 12, 12], replicated, may hold values from 38416 to 307328
- conv: float32 [9, 864], P(None, 'head'), may hold values from -1 to 1
- conv_m1: float32 [9, 864], P(None, 'head'), may hold values from -108.41586 to 108.41586
- conv_m2: float32 [9, 864], P(None, 'head'), may hold values from 653 to 5226
Outputs:
- output: float32 [32, 196, 216], P('dp')
- token_grad: float32 [32, 196, 216], P('dp')
- new_master: float32 [16, 54, 864], P('dp', None, 'head')
- new_master_m1: float32 [16, 54, 864], P('dp', None, 'head')
- new_master_m2: float32 [16, 54, 864], P('dp', None, 'head')
- master_copy: bfloat16 [16, 54, 864], P('dp', None, 'head')
- new_norm: float32 [4, 216], replicated
- new_norm_m1: float32 [4, 216], replicated
- new_norm_m2: float32 [4, 216], replicated
- new_talk: float32 [2, 12, 12], replicated
- new_talk_m1: float32 [2, 12, 12], replicated
- new_talk_m2: float32 [2, 12, 12], replicated
- new_conv: float32 [9, 864], P(None, 'head')
- new_conv_m1: float32 [9, 864], P(None, 'head')
- new_conv_m2: float32 [9, 864], P(None, 'head')
Inputs may be any that keep to these rules, and one draw needn't show every extreme that they name: `image_count`: image slots at or beyond a dp index's count are padding; some dp index holds exactly 4 images and some exactly 1. `block_slot`: the twelve slots are distinct.
All inputs are finite; a program needn't handle non-finite values.
Results may differ from a plain program's by a relative error of at most 0.012.
The roundings to bfloat16 on the way count: a program that leaves them out, or rounds other values in their place, can miss the bound.
Values may be sent and summed in bfloat16 or wider, within the bound.
No kernel may reach another device: no remote copies, remote signals or barrier semaphores. Data moves between devices by JAX's collectives and lax.ppermute only.
A program may use at most 64 MiB of HBM per device.

v0:
```python
import jax
import jax.numpy as jnp
from jax import lax
from jax.sharding import PartitionSpec as P

HD = 18
SIDE = 14
norm_eps = 1e-05
beta_first = 0.5
beta_second = 0.5
adam_eps = 1e-08
rate_matrix = 0.06
rate_small = 0.2
decay_matrix = 0.05
adam_steps = 3
highest = lax.Precision.HIGHEST


def normalize(values, gain_row, bias_row):
    centred = values - jnp.mean(values, axis=-1, keepdims=True)
    inverse = lax.rsqrt(jnp.mean(centred * centred, axis=-1, keepdims=True) + norm_eps)
    scaled = centred * inverse
    return (scaled, inverse, scaled * gain_row + bias_row)


def normalize_back(grad_normed, scaled, inverse, gain_row):
    grad_scaled = grad_normed * gain_row
    centred_grad = grad_scaled - jnp.mean(grad_scaled, axis=-1, keepdims=True)
    return inverse * (
        centred_grad - scaled * jnp.mean(grad_scaled * scaled, axis=-1, keepdims=True)
    )


def pad_grid(values):
    images, length, channels = values.shape
    return jnp.pad(values.reshape(images, SIDE, SIDE, channels), ((0, 0), (1, 1), (1, 1), (0, 0)))


def shifted(padded, row_off, col_off):
    return padded[:, 1 + row_off : 1 + row_off + SIDE, 1 + col_off : 1 + col_off + SIDE, :]


def conv_grid(hidden, kernel):
    padded = pad_grid(hidden)
    summed = jnp.zeros_like(shifted(padded, 0, 0))
    for tap_index in range(9):
        summed = summed + kernel[tap_index] * shifted(padded, tap_index // 3 - 1, tap_index % 3 - 1)
    return summed.reshape(hidden.shape)


def conv_back(grad_act, hidden, kernel):
    padded_grad = pad_grid(grad_act)
    padded_hidden = pad_grid(hidden)
    grad_grid = shifted(padded_grad, 0, 0)
    grad_hidden = jnp.zeros_like(grad_grid)
    kernel_rows = []
    for tap_index in range(9):
        row_off = tap_index // 3 - 1
        col_off = tap_index % 3 - 1
        grad_hidden = grad_hidden + kernel[tap_index] * shifted(padded_grad, -row_off, -col_off)
        kernel_rows.append(
            jnp.sum(grad_grid * shifted(padded_hidden, row_off, col_off), axis=(0, 1, 2))
        )
    return (grad_hidden.reshape(hidden.shape), jnp.stack(kernel_rows))


def mix_scores(received, talk):
    pre_mixed = jnp.einsum(
        "mn,gnqk->gmqk", talk[0], received.astype(jnp.float32), precision=highest
    )
    softmaxed = jax.nn.softmax(pre_mixed, axis=-1)
    post_mixed = jnp.einsum("jm,gmqk->gjqk", talk[1], softmaxed, precision=highest).astype(
        jnp.bfloat16
    )
    return (softmaxed, post_mixed)


def mix_back(grad_post_all, softmaxed, received, talk):
    grad_soft = jnp.einsum("jm,gjqk->gmqk", talk[1], grad_post_all, precision=highest)
    talk_post = jnp.einsum("gjqk,gmqk->jm", grad_post_all, softmaxed, precision=highest)
    grad_mixed = softmaxed * (grad_soft - jnp.sum(grad_soft * softmaxed, axis=-1, keepdims=True))
    talk_pre = jnp.einsum(
        "gmqk,gnqk->mn", grad_mixed, received.astype(jnp.float32), precision=highest
    )
    grad_scores = jnp.einsum("mn,gmqk->gnqk", talk[0], grad_mixed, precision=highest).astype(
        jnp.bfloat16
    )
    return (grad_scores, talk_pre, talk_post)


def adamw(weights_old, gradient, moment_one, moment_two, step_rate, decay_rate):
    one_new = beta_first * moment_one + (1.0 - beta_first) * gradient
    two_new = beta_second * moment_two + (1.0 - beta_second) * gradient * gradient
    hat_one = one_new / (1.0 - beta_first**adam_steps)
    hat_two = two_new / (1.0 - beta_second**adam_steps)
    weights_new = weights_old - step_rate * (
        hat_one / (jnp.sqrt(hat_two) + adam_eps) + decay_rate * weights_old
    )
    return (weights_new, one_new, two_new)


def gather_blocks(master, block_slot):
    mine = master.astype(jnp.bfloat16)
    data_devices = lax.axis_size("dp")
    every = lax.all_to_all(
        jnp.broadcast_to(mine[None], (data_devices,) + mine.shape),
        "dp",
        split_axis=0,
        concat_axis=0,
        tiled=True,
    )
    every = every.reshape((data_devices * mine.shape[0],) + mine.shape[1:])
    return jnp.take(every, block_slot, axis=0)


def split_pair(values):
    high = lax.reduce_precision(values, exponent_bits=8, mantissa_bits=7)
    low = values - high
    return jnp.concatenate([high.astype(jnp.bfloat16), low.astype(jnp.bfloat16)], axis=-2)


def join_pair(values):
    rows = values.shape[-2] // 2
    return values[..., :rows, :].astype(jnp.float32) + values[..., rows:, :].astype(jnp.float32)


def local(
    tokens,
    cotangent,
    image_count,
    subnet_heads,
    subnet_width,
    block_slot,
    master,
    master_m1,
    master_m2,
    norm_params,
    norm_m1,
    norm_m2,
    talk,
    talk_m1,
    talk_m2,
    conv,
    conv_m1,
    conv_m2,
):
    slot_count = master.shape[0]
    block_rows = master.shape[1]
    model_width = master.shape[2]
    capacity = tokens.shape[0]
    seq_len = tokens.shape[1]
    head_devices = lax.axis_size("head")
    data_devices = lax.axis_size("dp")
    head_place = lax.axis_index("head")
    images = capacity // head_devices
    heads = head_devices * (block_rows // HD)
    hidden_all = head_devices * 4 * block_rows
    scale_factor = HD ** (-0.5)
    first_image = head_place * images
    blocks = gather_blocks(master, block_slot)
    attn_blocks = lax.all_gather(blocks[0:4], "head", axis=0)
    ffn_blocks = lax.all_gather(blocks[4:12], "head", axis=0)
    conv_full = lax.all_gather(conv, "head", axis=1, tiled=True)
    w_query, w_key, w_value, w_out = [
        attn_blocks[:, i].reshape(head_devices * block_rows, model_width) for i in range(4)
    ]
    w_in = ffn_blocks[:, 0:4].reshape(hidden_all, model_width)
    w_down = ffn_blocks[:, 4:8].reshape(hidden_all, model_width)
    image_valid = (first_image + jnp.arange(images) < image_count[0]).astype(jnp.float32)
    head_keep = (jnp.arange(heads) < subnet_heads[0]).astype(jnp.float32)
    unit_keep = (jnp.arange(hidden_all) < subnet_width[0]).astype(jnp.float32)
    token_values = lax.dynamic_slice_in_dim(tokens, first_image, images, 0).astype(jnp.float32)
    my_cotangent = lax.dynamic_slice_in_dim(cotangent, first_image, images, 0)
    scaled_one, inverse_one, normed_full = normalize(token_values, norm_params[0], norm_params[1])
    normed_one = normed_full.astype(jnp.bfloat16)

    def project(weight):
        return (
            jnp.einsum("gsd,fd->gsf", normed_one, weight, preferred_element_type=jnp.float32)
            .astype(jnp.bfloat16)
            .reshape(images, seq_len, heads, HD)
        )

    queries, key_vecs, value_vecs = (project(w_query), project(w_key), project(w_value))
    scores = (
        jnp.einsum("gqhe,gkhe->ghqk", queries, key_vecs, preferred_element_type=jnp.float32)
        * scale_factor
    ).astype(jnp.bfloat16)
    softmaxed, post_mixed = mix_scores(scores, talk)
    attended = (
        jnp.einsum("ghqk,gkhe->gqhe", post_mixed, value_vecs, preferred_element_type=jnp.float32)
        * head_keep[None, None, :, None]
    )
    attended = attended.astype(jnp.bfloat16).reshape(images, seq_len, heads * HD)
    middle = token_values + jnp.einsum(
        "gsf,fd->gsd", attended, w_out, preferred_element_type=jnp.float32
    )
    scaled_two, inverse_two, normed_full_two = normalize(middle, norm_params[2], norm_params[3])
    normed_two = normed_full_two.astype(jnp.bfloat16)
    hidden = jnp.einsum("gsd,ud->gsu", normed_two, w_in, preferred_element_type=jnp.float32)
    activated = conv_grid(hidden, conv_full)
    sigmoid_act = jax.nn.sigmoid(activated)
    gated = (activated * sigmoid_act * unit_keep).astype(jnp.bfloat16)
    down = jnp.einsum("gsu,ud->gsd", gated, w_down, preferred_element_type=jnp.float32)
    my_output = (middle + down) * image_valid[:, None, None]
    output = lax.all_gather(my_output.astype(jnp.bfloat16), "head", axis=0, tiled=True).astype(
        jnp.float32
    )
    grad_output = my_cotangent * image_valid[:, None, None]
    grad_low = grad_output.astype(jnp.bfloat16)
    grad_down = jnp.einsum("gsu,gsd->ud", gated, grad_low, preferred_element_type=jnp.float32)
    grad_gated = (
        jnp.einsum("gsd,ud->gsu", grad_low, w_down, preferred_element_type=jnp.float32) * unit_keep
    )
    grad_act = grad_gated * sigmoid_act * (1.0 + activated * (1.0 - sigmoid_act))
    grad_hidden, grad_kernel = conv_back(grad_act, hidden, conv_full)
    grad_hidden_low = grad_hidden.astype(jnp.bfloat16)
    grad_in = jnp.einsum(
        "gsu,gsd->ud", grad_hidden_low, normed_two, preferred_element_type=jnp.float32
    )
    grad_normed_two = jnp.einsum(
        "gsu,ud->gsd", grad_hidden_low, w_in, preferred_element_type=jnp.float32
    )
    grad_middle = grad_output + normalize_back(
        grad_normed_two, scaled_two, inverse_two, norm_params[2]
    )
    grad_branch = grad_middle.astype(jnp.bfloat16)
    grad_out_proj = jnp.einsum(
        "gsf,gsd->fd", attended, grad_branch, preferred_element_type=jnp.float32
    )
    grad_attended = jnp.einsum(
        "gsd,fd->gsf", grad_branch, w_out, preferred_element_type=jnp.float32
    ).reshape(images, seq_len, heads, HD)
    grad_att_low = (grad_attended * head_keep[None, None, :, None]).astype(jnp.bfloat16)
    grad_values = jnp.einsum(
        "ghqk,gqhe->gkhe", post_mixed, grad_att_low, preferred_element_type=jnp.float32
    ).astype(jnp.bfloat16)
    grad_post = jnp.einsum(
        "gqhe,gkhe->ghqk", grad_att_low, value_vecs, preferred_element_type=jnp.float32
    ).astype(jnp.bfloat16)
    grad_scores, talk_pre, talk_post = mix_back(
        grad_post.astype(jnp.float32), softmaxed, scores, talk
    )
    grad_queries = (
        jnp.einsum("ghqk,gkhe->gqhe", grad_scores, key_vecs, preferred_element_type=jnp.float32)
        * scale_factor
    ).astype(jnp.bfloat16)
    grad_keys = (
        jnp.einsum("ghqk,gqhe->gkhe", grad_scores, queries, preferred_element_type=jnp.float32)
        * scale_factor
    ).astype(jnp.bfloat16)
    grad_parts = [
        part.reshape(images, seq_len, heads * HD) for part in (grad_queries, grad_keys, grad_values)
    ]
    grad_projs = [
        jnp.einsum("gsf,gsd->fd", part, normed_one, preferred_element_type=jnp.float32)
        for part in grad_parts
    ]
    grad_normed_one = sum(
        (
            jnp.einsum("gsf,fd->gsd", part, weight, preferred_element_type=jnp.float32)
            for part, weight in zip(grad_parts, (w_query, w_key, w_value))
        )
    )
    my_token_grad = grad_middle + normalize_back(
        grad_normed_one, scaled_one, inverse_one, norm_params[0]
    )
    token_grad = lax.all_gather(
        my_token_grad.astype(jnp.bfloat16), "head", axis=0, tiled=True
    ).astype(jnp.float32)
    norm_part = jnp.stack(
        [
            jnp.sum(grad_normed_one * scaled_one, axis=(0, 1)),
            jnp.sum(grad_normed_one, axis=(0, 1)),
            jnp.sum(grad_normed_two * scaled_two, axis=(0, 1)),
            jnp.sum(grad_normed_two, axis=(0, 1)),
        ]
    )
    talk_part = jnp.stack([talk_pre, talk_post]).reshape(2, heads * heads)
    talk_part = jnp.pad(talk_part, ((0, 0), (0, model_width - heads * heads)))
    every_head = jnp.broadcast_to(
        jnp.concatenate([norm_part, talk_part])[None], (head_devices, 6, model_width)
    )
    conv_part = grad_kernel.reshape(9, head_devices, model_width).transpose(1, 0, 2)
    small = split_pair(jnp.concatenate([every_head, conv_part], axis=1))

    def by_head(matrix):
        return matrix.reshape(head_devices, -1, model_width)

    message = jnp.concatenate(
        [by_head(m).astype(jnp.bfloat16) for m in (*grad_projs, grad_out_proj, grad_in, grad_down)]
        + [small],
        axis=1,
    )
    received = lax.all_to_all(message, "head", split_axis=0, concat_axis=0, tiled=True)
    matrix_rows = 12 * block_rows
    block_grads = jnp.sum(received[:, :matrix_rows].astype(jnp.float32), axis=0).reshape(
        12, block_rows, model_width
    )
    small_sum = jnp.sum(join_pair(received[:, matrix_rows:]), axis=0)
    all_slots = slot_count * data_devices
    spread_grads = (
        jnp.zeros((all_slots, block_rows, model_width), jnp.bfloat16)
        .at[block_slot]
        .set(block_grads.astype(jnp.bfloat16))
        .reshape(data_devices, slot_count * block_rows, model_width)
    )
    small_pair = split_pair(small_sum)
    message_two = jnp.concatenate(
        [spread_grads, jnp.broadcast_to(small_pair[None], (data_devices,) + small_pair.shape)],
        axis=1,
    )
    received_two = lax.all_to_all(message_two, "dp", split_axis=0, concat_axis=0, tiled=True)
    slot_rows = slot_count * block_rows
    slot_grads = jnp.sum(received_two[:, :slot_rows].astype(jnp.float32), axis=0).reshape(
        slot_count, block_rows, model_width
    )
    small_total = jnp.sum(join_pair(received_two[:, slot_rows:]), axis=0)
    norm_grad = small_total[0:4]
    talk_grad = small_total[4:6, : heads * heads].reshape(2, heads, heads)
    conv_grad = small_total[6:15]
    new_master, new_master_m1, new_master_m2 = adamw(
        master, slot_grads, master_m1, master_m2, rate_matrix, decay_matrix
    )
    new_norm, new_norm_m1, new_norm_m2 = adamw(
        norm_params, norm_grad, norm_m1, norm_m2, rate_small, 0.0
    )
    new_talk, new_talk_m1, new_talk_m2 = adamw(talk, talk_grad, talk_m1, talk_m2, rate_small, 0.0)
    new_conv, new_conv_m1, new_conv_m2 = adamw(
        conv, conv_grad, conv_m1, conv_m2, rate_small, decay_matrix
    )
    return (
        output,
        token_grad,
        new_master,
        new_master_m1,
        new_master_m2,
        new_master.astype(jnp.bfloat16),
        new_norm,
        new_norm_m1,
        new_norm_m2,
        new_talk,
        new_talk_m1,
        new_talk_m2,
        new_conv,
        new_conv_m1,
        new_conv_m2,
    )


def solution(mesh):
    in_specs = (
        P("dp", None, None),
        P("dp", None, None),
        P("dp"),
        P(),
        P(),
        P(),
        P("dp", None, "head"),
        P("dp", None, "head"),
        P("dp", None, "head"),
        P(),
        P(),
        P(),
        P(),
        P(),
        P(),
        P(None, "head"),
        P(None, "head"),
        P(None, "head"),
    )
    out_specs = (
        P("dp", None, None),
        P("dp", None, None),
        P("dp", None, "head"),
        P("dp", None, "head"),
        P("dp", None, "head"),
        P("dp", None, "head"),
        P(),
        P(),
        P(),
        P(),
        P(),
        P(),
        P(None, "head"),
        P(None, "head"),
        P(None, "head"),
    )
    return jax.shard_map(local, mesh=mesh, in_specs=in_specs, out_specs=out_specs, check_vma=False)
```

profile of v0, /device:TPU:0, one launch (start us, length us, event | category | flops | bytes accessed | tf_op | source)
XLA Modules:
  0.0 175.3 jit_solution(16513780593674227736)
XLA Ops:
  0.7 1.0 convert_element_type.208
  1.7 1.0 broadcast_in_dim.21
  2.7 7.3 %all-to-all-start = ((bf16[8,2,54,216]{3,1,2,0:T(2,128)(2,1)}), bf16[8,2,54,216]{3,1,2,0:T(2,128)(2,1)S(1)}, u32[]{:S(2)}, u32[]{:S(2)}) async-start(bf16[8,2,54,216]{3,1,2,0:T(2,128)(2,1)} %broadcast_in_dim.21), calls=%async_computation | async-start | bytes 884736 | tf_op jit(solution)/shard_map/all_to_all | solution.py:105
  13.3 5.4 %all-gather.2 = f32[4,216,9]{1,2,0:T(8,128)S(1)} all-gather(f32[1,216,9]{1,2,0:T(8,128)} %bitcast.275), channel_id=1, replica_groups=mesh['dp'=8,'head'=4] {'head'}, dimensions={0}, use_global_device_ids=true | all-gather | bytes 38880 | tf_op jit(solution)/shard_map/all_gather | solution.py:163
  19.8 1.2 constant_dynamic-slice_fusion.1
  23.7 6.9 %all-gather = bf16[16,54,216]{2,1,0:T(8,128)(2,1)S(1)} all-gather(bf16[4,54,216]{2,1,0:T(8,128)(2,1)S(1)} %slice.225), channel_id=2, replica_groups=mesh['dp'=8,'head'=4] {'head'}, dimensions={0}, use_global_device_ids=true | all-gather | bytes 466560 | tf_op jit(solution)/shard_map/all_gather | solution.py:161
  33.6 9.3 %all-gather.1 = bf16[32,54,216]{2,0,1:T(8,128)(2,1)S(1)} all-gather(bf16[8,54,216]{2,0,1:T(8,128)(2,1)S(1)} %copy.283), channel_id=3, replica_groups=mesh['dp'=8,'head'=4] {'head'}, dimensions={0}, use_global_device_ids=true | all-gather | bytes 933120 | tf_op jit(solution)/shard_map/all_gather | solution.py:162
  43.3 1.0 reshape.508
  45.2 2.0 %bitcast_reduce_fusion = (f32[12,196]{0,1:T(8,128)S(1)}, f32[196,196,12]{1,2,0:T(8,128)S(1)}) fusion(f32[2,12,12]{2,1,0:T(8,128)S(1)} %copy.278, bf16[12,196,196]{2,1,0:T(8,128)(2,1)S(1)} %multiply_convert_fusion), kind=kOutput, calls=%fused_computation.15 | convolution fusion | flops 66841488 | bytes 3090368 | tf_op jit(solution)/shard_map/mn,gnqk->gmqk/dot_general | solution.py:68
  47.2 1.1 fusion.12
  48.9 3.9 %fusion.28 = bf16[12,196,196]{2,0,1:T(8,128)(2,1)S(1)} fusion(f32[2,12,12]{2,1,0:T(8,128)S(1)} %copy.278, f32[196,196,12]{1,2,0:T(8,128)S(1)} %get-tuple-element.163, f32[12,196]{0,1:T(8,128)S(1)} %fusion.12, f32[12,196]{0,1:T(8,128)S(1)} %get-tuple-element.162), kind=kOutput, calls=%fused_computation.30 | convolution fusion | flops 67765824 | bytes 4346240 | tf_op jit(solution)/shard_map/jm,gmqk->gjqk/dot_general | solution.py:72
  52.9 1.2 copy-done.3
  55.2 1.2 fusion.111
  56.4 1.2 reshape.507
  57.6 1.8 %multiply_convert_fusion.1 = (bf16[1,14,14,864]{3,2,1,0:T(8,128)(2,1)}, f32[1,14,14,864]{3,2,1,0:T(8,128)}) fusion(f32[864]{0:T(1024)S(1)} %fusion.125, f32[864]{0:T(1024)S(1)} %get-tuple-element.122, f32[864]{0:T(1024)S(1)} %get-tuple-element.123, f32[864]{0:T(1024)S(1)} %get-tuple-element.124, f32[864]{0:T(1024)S(1)} %get-tuple-element.125, ...), kind=kLoop, calls=%fused_computation.114 | loop fusion | flops 3894912 | bytes 1728000 | tf_op jit(solution)/shard_map/convert_element_type | solution.py:203
  59.4 2.1 %reshape.510 = f32[196,864]{1,0:T(8,128)} reshape(f32[1,14,14,864]{3,2,1,0:T(8,128)} %get-tuple-element.144) | data formatting | bytes 1354752 | tf_op jit(solution)/shard_map/reshape | solution.py:48
  61.5 2.0 %fusion.81 = bf16[864,196]{0,1:T(8,128)(2,1)} fusion(f32[864]{0:T(1024)S(1)} %fusion.125, f32[196,864]{1,0:T(8,128)} %reshape.510), kind=kLoop, calls=%fused_computation.123 | loop fusion | flops 1016064 | bytes 1019520 | tf_op jit(solution)/shard_map/gsu,gsd->ud/dot_general | solution.py:211
  63.5 3.5 %multiply_reduce_fusion.8 = (f32[864]{0:T(1024)}, f32[196,864]{1,0:T(8,128)}) fusion(f32[196,864]{1,0:T(8,128)} %fusion.111, f32[196,864]{1,0:T(8,128)} %reshape.510, f32[864]{0:T(1024)S(1)} %fusion.125, bf16[864,216]{1,0:T(8,128)(2,1)} %reshape.508, f32[]{:T(128)} %bitcast.30, f32[1,196,216]{2,0,1:T(1,128)} %constant_dynamic-slice_fusion), kind=kOutput, calls=%fused_computation.116 | convolution fusion | flops 75103200 | bytes 2581636 | tf_op jit(solution)/shard_map/gsd,ud->gsu/dot_general | solution.py:213
  67.0 2.1 %reshape.511 = f32[1,14,14,864]{3,2,1,0:T(8,128)} reshape(f32[196,864]{1,0:T(8,128)} %get-tuple-element.171) | data formatting | bytes 1354752 | tf_op jit(solution)/shard_map/reshape | solution.py:36
  69.1 7.3 %multiply_reduce_fusion = (f32[864]{0:T(1024)}, f32[864]{0:T(1024)}, f32[864]{0:T(1024)}, f32[864]{0:T(1024)}, f32[864]{0:T(1024)}, /*index=5*/f32[864]{0:T(1024...) fusion(f32[1,14,14,864]{3,2,1,0:T(8,128)} %reshape.511, f32[1,14,14,864]{3,2,1,0:T(8,128)S(1)} %reshape.507, ...), kind=kLoop, calls=%fused_computation.106 | loop fusion | flops 5750784 | bytes 1752192 | tf_op jit(solution)/shard_map/reduce_sum | solution.py:62
  76.4 1.2 convert_element_type.227
  77.6 1.8 %fusion.97 = (f32[216]{0:T(256)}, f32[196]{0:T(256)S(1)}, f32[196,216]{1,0:T(8,128)S(1)}) fusion(f32[1,196,216]{2,1,0:T(8,128)S(1)} %get-tuple-element.165, f32[196]{0:T(256)} %copy-done.34, f32[196]{0:T(256)} %copy-done.30, f32[216]{0:T(256)} %bitcast.278, bf16[196,864]{1,0:T(8,128)(2,1)S(1)} %convert_element_type.227, bf16[864,216]{1,0:T(8,128)(2,1)S(1)} %reshape.506), kind=kOutput, calls=%fused_computation.144 | convolution fusion | flops 73452544 | bytes 1054704 | tf_op jit(solution)/shard_map/gsu,ud->gsd/dot_general | solution.py:221
  79.4 1.3 fusion.136
  80.7 1.1 fusion.100
  81.8 1.1 fusion.36
  82.9 1.9 %fusion.44 = bf16[1,196,12,18]{1,3,2,0:T(8,128)(2,1)S(1)} fusion(bf16[196,12,18]{0,2,1:T(8,128)(2,1)S(1)} %fusion.36, bf16[12,196,196]{2,0,1:T(8,128)(2,1)} %copy-done.3), kind=kOutput, calls=%fused_computation.62 | convolution fusion | flops 16638048 | bytes 1091328 | tf_op jit(solution)/shard_map/ghqk,gqhe->gkhe/dot_general | solution.py:235
  85.4 3.4 %fusion.48 = f32[12,12]{1,0:T(8,128)} fusion(bf16[12,196,196]{2,1,0:T(8,128)(2,1)S(1)} %convolution_convert_fusion, f32[196,196,12]{1,2,0:T(8,128)S(1)} %copy-done.2, f32[12,196]{0,1:T(8,128)S(1)} %copy-done.27, f32[12,196]{0,1:T(8,128)S(1)} %copy-done.23), kind=kOutput, calls=%fused_computation.66 | convolution fusion | flops 67304832 | bytes 2785344 | tf_op jit(solution)/shard_map/gjqk,gmqk->jm/dot_general | solution.py:80
  88.8 4.1 %fusion.4 = (f32[12,196]{0,1:T(8,128)S(1)}, f32[196,196,12]{1,2,0:T(8,128)S(1)}) fusion(f32[12,196]{0,1:T(8,128)S(1)} %copy-done.27, f32[12,196]{0,1:T(8,128)S(1)} %copy-done.23, f32[196,196,12]{1,2,0:T(8,128)S(1)} %copy-done.2, f32[2,12,12]{2,1,0:T(8,128)S(1)} %copy.278, bf16[12,196,196]{2,1,0:T(8,128)(2,1)S(1)} %convolution_convert_fusion), kind=kOutput, calls=%fused_computation.8 | convolution fusion | flops 68224464 | bytes 6506432 | tf_op jit(solution)/shard_map/jm,gjqk->gmqk/dot_general | solution.py:79
  92.9 3.8 %fusion.53 = f32[12,12]{1,0:T(8,128)} fusion(bf16[12,196,196]{2,1,0:T(8,128)(2,1)S(1)} %multiply_convert_fusion, f32[12,196]{0,1:T(8,128)S(1)} %get-tuple-element.167, f32[196,196,12]{1,2,0:T(8,128)S(1)} %get-tuple-element.168, f32[196,196,12]{1,2,0:T(8,128)S(1)} %copy-done.2, f32[12,196]{0,1:T(8,128)S(1)} %copy-done.27, f32[12,196]{0,1:T(8,128)S(1)} %copy-done.23), kind=kOutput, calls=%fused_computation.67 | convolution fusion | flops 68226816 | bytes 4638720 | tf_op jit(solution)/shard_map/gmqk,gnqk->mn/dot_general | solution.py:82
  96.7 4.7 %fusion.25 = bf16[12,196,196]{2,0,1:T(8,128)(2,1)S(1)} fusion(f32[196,196,12]{1,2,0:T(8,128)S(1)} %get-tuple-element.168, f32[12,196]{0,1:T(8,128)S(1)} %get-tuple-element.167, f32[2,12,12]{2,1,0:T(8,128)S(1)} %copy.278, f32[196,196,12]{1,2,0:T(8,128)S(1)} %copy-done.2, f32[12,196]{0,1:T(8,128)S(1)} %copy-done.27, f32[12,196]{0,1:T(8,128)S(1)} %copy-done.23), kind=kOutput, calls=%fused_computation.29 | convolution fusion | flops 68687808 | bytes 7659904 | tf_op jit(solution)/shard_map/mn,gmqk->gnqk/dot_general | solution.py:85
  101.6 1.1 fusion.45
  102.8 1.1 fusion.46
  107.2 1.1 copy.301
  110.4 1.0 reshape.516
  111.4 1.1 fusion.147
  112.5 1.1 convolution_add_fusion.1
  113.6 1.2 fusion.95
  119.3 3.8 %concatenate.19 = bf16[4,678,216]{1,2,0:T(8,128)(2,1)} concatenate(bf16[4,54,216]{1,2,0:T(8,128)(2,1)S(1)} %copy.298, bf16[4,54,216]{1,2,0:T(8,128)(2,1)} %copy.299, bf16[4,54,216]{1,2,0:T(8,128)(2,1)} %copy.300, bf16[4,54,216]{1,2,0:T(8,128)(2,1)S(1)} %copy.301, bf16[4,216,216]{1,2,0:T(8,128)(2,1)S(1)} %convolution_convert_fusion.2, ...), dimensions={1} | concatenate | bytes 2343168 | tf_op jit(solution)/shard_map/concatenate | solution.py:290
  123.1 3.5 %all-to-all-start.1 = ((bf16[4,678,216]{1,2,0:T(8,128)(2,1)}), bf16[4,678,216]{1,2,0:T(8,128)(2,1)S(1)}, u32[]{:S(2)}, u32[]{:S(2)}) async-start(bf16[4,678,216]{1,2,0:T(8,128)(2,1)} %concatenate.19), calls=%async_computation.1 | async-start | bytes 2654208 | tf_op jit(solution)/shard_map/all_to_all | solution.py:295
  126.6 1.9 %convert_element_type.222 = bf16[196,864]{1,0:T(8,128)(2,1)} reshape(bf16[1,14,14,864]{3,2,1,0:T(8,128)(2,1)} %get-tuple-element.143) | data formatting | bytes 677376 | tf_op jit(solution)/shard_map/convert_element_type | solution.py:203
  128.5 1.3 fusion.43
  129.8 14.2 %all-to-all-done.1 = bf16[4,678,216]{1,2,0:T(8,128)(2,1)S(1)} async-done(((bf16[4,678,216]{1,2,0:T(8,128)(2,1)}), bf16[4,678,216]{1,2,0:T(8,128)(2,1)S(1)}, u32[]{:S(2)}, u32[]{:S(2)}) %all-to-all-start.1) | async-done | bytes 1171616 | tf_op jit(solution)/shard_map/all_to_all | solution.py:295
  144.9 1.1 scatter_fusion
  147.2 6.1 %all-to-all-start.2 = ((bf16[8,138,216]{2,1,0:T(8,128)(2,1)}), bf16[8,138,216]{2,1,0:T(8,128)(2,1)S(1)}, u32[]{:S(2)}, u32[]{:S(2)}) async-start(bf16[8,138,216]{2,1,0:T(8,128)(2,1)} %pad_maximum_fusion), calls=%async_computation.2 | async-start | bytes 1179648 | tf_op jit(solution)/shard_map/all_to_all | solution.py:313
  153.3 6.2 %all_gather.26 = bf16[4,196,216]{2,1,0:T(8,128)(2,1)S(1)} all-gather(bf16[1,196,216]{2,1,0:T(8,128)(2,1)S(1)} %fusion.43), channel_id=1, replica_groups=mesh['dp'=8,'head'=4] {'head'}, dimensions={0}, use_global_device_ids=true | all-gather | bytes 423360 | tf_op jit(solution)/shard_map/all_gather | solution.py:206
  159.5 1.0 copy.314
  160.7 6.7 %all_gather.27 = bf16[4,196,216]{2,1,0:T(8,128)(2,1)S(1)} all-gather(bf16[1,196,216]{2,1,0:T(8,128)(2,1)S(1)} %fusion.94), channel_id=1, replica_groups=mesh['dp'=8,'head'=4] {'head'}, dimensions={0}, use_global_device_ids=true | all-gather | bytes 423360 | tf_op jit(solution)/shard_map/all_gather | solution.py:268
  167.4 1.0 copy.315
  (262 shorter events, 29.9 us)
Async XLA Ops:
  0.6 18.3 %copy-start = (f32[4,196,216]{2,0,1:T(4,128)S(1)}, f32[4,196,216]{2,0,1:T(4,128)}, u32[]{:S(2)}) copy-start(f32[4,196,216]{2,0,1:T(4,128)} %param.19) | copy-start | bytes 2032132
  2.7 20.2 %all-to-all-start = ((bf16[8,2,54,216]{3,1,2,0:T(2,128)(2,1)}), bf16[8,2,54,216]{3,1,2,0:T(2,128)(2,1)S(1)}, u32[]{:S(2)}, u32[]{:S(2)}) async-start(bf16[8,2,54,216]{3,1,2,0:T(2,128)(2,1)} %broadcast_in_dim.21), calls=%async_computation | async-start | bytes 884736 | tf_op jit(solution)/shard_map/all_to_all | solution.py:105
  11.9 41.0 %copy-start.66 = (f32[12]{0:T(128)}, f32[12]{0:T(128)S(1)}, u32[]{:S(2)}) copy-start(f32[12]{0:T(128)S(1)} %compare_convert_fusion) | copy-start | bytes 148
  12.6 18.9 %copy-start.64 = (s32[12]{0:T(128)}, s32[12]{0:T(128)S(1)}, u32[]{:S(2)}) copy-start(s32[12]{0:T(128)S(1)} %compare_select_fusion) | copy-start | bytes 148
  21.1 33.5 %copy-start.4 = (bf16[1,196,216]{2,1,0:T(8,128)(2,1)}, bf16[1,196,216]{2,1,0:T(8,128)(2,1)S(1)}, u32[]{:S(2)}) copy-start(bf16[1,196,216]{2,1,0:T(8,128)(2,1)S(1)} %get-tuple-element.146) | copy-start | bytes 254020
  21.2 11.3 %copy-start.36 = (f32[196]{0:T(256)}, f32[196]{0:T(256)S(1)}, u32[]{:S(2)}) copy-start(f32[196]{0:T(256)S(1)} %broadcast_multiply_fusion.5) | copy-start | bytes 2356
  22.0 10.5 %copy-start.53 = (f32[196]{0:T(256)}, f32[196]{0:T(256)S(1)}, u32[]{:S(2)}) copy-start(f32[196]{0:T(256)S(1)} %add_rsqrt_fusion.1) | copy-start | bytes 2356
  22.9 9.6 %copy-start.38 = (f32[1,216]{1,0:T(1,128)}, f32[1,216]{1,0:T(1,128)S(1)}, u32[]{:S(2)}) copy-start(f32[1,216]{1,0:T(1,128)S(1)} %get-tuple-element.160) | copy-start | bytes 2596
  22.9 9.6 %copy-start.67 = (f32[1,216]{1,0:T(1,128)}, f32[1,216]{1,0:T(1,128)S(1)}, u32[]{:S(2)}) copy-start(f32[1,216]{1,0:T(1,128)S(1)} %get-tuple-element.159) | copy-start | bytes 2596
  22.9 32.3 %copy-start.32 = (f32[1,216]{1,0:T(1,128)}, f32[1,216]{1,0:T(1,128)S(1)}, u32[]{:S(2)}) copy-start(f32[1,216]{1,0:T(1,128)S(1)} %get-tuple-element.158) | copy-start | bytes 2596
  22.9 32.3 %copy-start.55 = (f32[1,216]{1,0:T(1,128)}, f32[1,216]{1,0:T(1,128)S(1)}, u32[]{:S(2)}) copy-start(f32[1,216]{1,0:T(1,128)S(1)} %get-tuple-element.161) | copy-start | bytes 2596
  31.5 11.6 %copy-start.18 = (bf16[216,216]{1,0:T(8,128)(2,1)}, bf16[216,216]{1,0:T(8,128)(2,1)S(1)}, u32[]{:S(2)}) copy-start(bf16[216,216]{1,0:T(8,128)(2,1)S(1)} %reshape_squeeze.14) | copy-start | bytes 279940
  31.9 12.7 %copy-start.9 = (bf16[196,12,18]{0,2,1:T(8,128)(2,1)}, bf16[196,12,18]{0,2,1:T(8,128)(2,1)S(1)}, u32[]{:S(2)}) copy-start(bf16[196,12,18]{0,2,1:T(8,128)(2,1)S(1)} %reshape.501) | copy-start | bytes 254020
  32.0 11.1 %copy-start.20 = (bf16[216,216]{1,0:T(8,128)(2,1)}, bf16[216,216]{1,0:T(8,128)(2,1)S(1)}, u32[]{:S(2)}) copy-start(bf16[216,216]{1,0:T(8,128)(2,1)S(1)} %reshape_squeeze.13) | copy-start | bytes 279940
  32.4 12.2 %copy-start.11 = (bf16[196,12,18]{0,2,1:T(8,128)(2,1)}, bf16[196,12,18]{0,2,1:T(8,128)(2,1)S(1)}, u32[]{:S(2)}) copy-start(bf16[196,12,18]{0,2,1:T(8,128)(2,1)S(1)} %reshape.500) | copy-start | bytes 254020
  33.6 19.3 %copy-start.13 = (bf16[196,12,18]{0,2,1:T(8,128)(2,1)}, bf16[196,12,18]{0,2,1:T(8,128)(2,1)S(1)}, u32[]{:S(2)}) copy-start(bf16[196,12,18]{0,2,1:T(8,128)(2,1)S(1)} %reshape.499) | copy-start | bytes 254020
  47.1 5.7 %copy-start.1 = (f32[196,196,12]{1,2,0:T(8,128)}, f32[196,196,12]{1,2,0:T(8,128)S(1)}, u32[]{:S(2)}) copy-start(f32[196,196,12]{1,2,0:T(8,128)S(1)} %get-tuple-element.163) | copy-start | bytes 5531908
  47.1 5.7 %copy-start.22 = (f32[12,196]{0,1:T(8,128)}, f32[12,196]{0,1:T(8,128)S(1)}, u32[]{:S(2)}) copy-start(f32[12,196]{0,1:T(8,128)S(1)} %get-tuple-element.162) | copy-start | bytes 28228
  54.9 6.5 %copy-start.30 = (f32[196]{0:T(256)}, f32[196]{0:T(256)S(1)}, u32[]{:S(2)}) copy-start(f32[196]{0:T(256)S(1)} %broadcast_multiply_fusion.4) | copy-start | bytes 2356
  55.1 6.3 %copy-start.34 = (f32[196]{0:T(256)}, f32[196]{0:T(256)S(1)}, u32[]{:S(2)}) copy-start(f32[196]{0:T(256)S(1)} %add_rsqrt_fusion) | copy-start | bytes 2356
  76.4 8.5 %copy-start.14 = (bf16[196,12,18]{0,2,1:T(8,128)(2,1)S(1)}, bf16[196,12,18]{0,2,1:T(8,128)(2,1)}, u32[]{:S(2)}) copy-start(bf16[196,12,18]{0,2,1:T(8,128)(2,1)} %copy-done.13) | copy-start | bytes 254020
  76.4 9.0 %copy-start.23 = (f32[12,196]{0,1:T(8,128)S(1)}, f32[12,196]{0,1:T(8,128)}, u32[]{:S(2)}) copy-start(f32[12,196]{0,1:T(8,128)} %copy-done.22) | copy-start | bytes 28228
  76.4 9.0 %copy-start.27 = (f32[12,196]{0,1:T(8,128)S(1)}, f32[12,196]{0,1:T(8,128)}, u32[]{:S(2)}) copy-start(f32[12,196]{0,1:T(8,128)} %copy-done.26) | copy-start | bytes 28228
  77.6 7.8 %copy-start.2 = (f32[196,196,12]{1,2,0:T(8,128)S(1)}, f32[196,196,12]{1,2,0:T(8,128)}, u32[]{:S(2)}) copy-start(f32[196,196,12]{1,2,0:T(8,128)} %copy-done.1) | copy-start | bytes 5531908
  96.7 6.1 %copy-start.10 = (bf16[196,12,18]{0,2,1:T(8,128)(2,1)S(1)}, bf16[196,12,18]{0,2,1:T(8,128)(2,1)}, u32[]{:S(2)}) copy-start(bf16[196,12,18]{0,2,1:T(8,128)(2,1)} %copy-done.9) | copy-start | bytes 254020
  96.7 7.2 %copy-start.16 = (bf16[196,216]{0,1:T(8,128)(2,1)S(1)}, bf16[196,216]{0,1:T(8,128)(2,1)}, u32[]{:S(2)}) copy-start(bf16[196,216]{0,1:T(8,128)(2,1)} %copy-done.15) | copy-start | bytes 254020
  103.9 6.3 %copy-start.57 = (f32[12,12]{1,0:T(8,128)S(1)}, f32[12,12]{1,0:T(8,128)}, u32[]{:S(2)}) copy-start(f32[12,12]{1,0:T(8,128)} %fusion.48) | copy-start | bytes 1732
  103.9 6.3 %copy-start.58 = (f32[12,12]{1,0:T(8,128)S(1)}, f32[12,12]{1,0:T(8,128)}, u32[]{:S(2)}) copy-start(f32[12,12]{1,0:T(8,128)} %fusion.53) | copy-start | bytes 1732
  104.8 5.6 %copy-start.17 = (bf16[1,196,12,18]{1,3,2,0:T(8,128)(2,1)S(1)}, bf16[1,196,12,18]{1,3,2,0:T(8,128)(2,1)}, u32[]{:S(2)}) copy-start(bf16[1,196,12,18]{1,3,2,0:T(8,128)(2,1)} %fusion.46) | copy-start | bytes 254020
  107.2 9.0 %copy-start.68 = (f32[1,216]{1,0:T(1,128)S(1)}, f32[1,216]{1,0:T(1,128)}, u32[]{:S(2)}) copy-start(f32[1,216]{1,0:T(1,128)} %copy-done.67) | copy-start | bytes 2596
  107.2 10.3 %copy-start.59 = (f32[216]{0:T(256)S(1)}, f32[216]{0:T(256)}, u32[]{:S(2)}) copy-start(f32[216]{0:T(256)} %get-tuple-element.117) | copy-start | bytes 2596
  107.2 10.3 %copy-start.63 = (f32[216]{0:T(256)S(1)}, f32[216]{0:T(256)}, u32[]{:S(2)}) copy-start(f32[216]{0:T(256)} %get-tuple-element.113) | copy-start | bytes 2596
  119.3 9.2 %copy-start.7 = (bf16[864,216]{1,0:T(8,128)(2,1)S(1)}, bf16[864,216]{1,0:T(8,128)(2,1)}, u32[]{:S(2)}) copy-start(bf16[864,216]{1,0:T(8,128)(2,1)} %reshape.508) | copy-start | bytes 1119748
  123.1 21.0 %all-to-all-start.1 = ((bf16[4,678,216]{1,2,0:T(8,128)(2,1)}), bf16[4,678,216]{1,2,0:T(8,128)(2,1)S(1)}, u32[]{:S(2)}, u32[]{:S(2)}) async-start(bf16[4,678,216]{1,2,0:T(8,128)(2,1)} %concatenate.19), calls=%async_computation.1 | async-start | bytes 2654208 | tf_op jit(solution)/shard_map/all_to_all | solution.py:295
  126.6 18.2 %copy-start.65 = (s32[12]{0:T(128)S(1)}, s32[12]{0:T(128)}, u32[]{:S(2)}) copy-start(s32[12]{0:T(128)} %copy-done.64) | copy-start | bytes 148
  147.1 22.1 %copy-start.29 = (f32[2,12,12]{2,0,1:T(2,128)S(1)}, f32[2,12,12]{2,0,1:T(2,128)}, u32[]{:S(2)}) copy-start(f32[2,12,12]{2,0,1:T(2,128)} %param.30) | copy-start | bytes 3460
  147.1 22.1 %copy-start.51 = (f32[2,12,12]{2,0,1:T(2,128)S(1)}, f32[2,12,12]{2,0,1:T(2,128)}, u32[]{:S(2)}) copy-start(f32[2,12,12]{2,0,1:T(2,128)} %param.31) | copy-start | bytes 3460
  147.1 22.1 %copy-start.52 = (f32[2,12,12]{2,0,1:T(2,128)S(1)}, f32[2,12,12]{2,0,1:T(2,128)}, u32[]{:S(2)}) copy-start(f32[2,12,12]{2,0,1:T(2,128)} %param.32) | copy-start | bytes 3460
  147.1 24.0 %copy-start.19 = (f32[2,54,216]{2,0,1:T(2,128)S(1)}, f32[2,54,216]{2,0,1:T(2,128)}, u32[]{:S(2)}) copy-start(f32[2,54,216]{2,0,1:T(2,128)} %param.24) | copy-start | bytes 279940
  147.1 24.0 %copy-start.24 = (f32[2,54,216]{2,0,1:T(2,128)S(1)}, f32[2,54,216]{2,0,1:T(2,128)}, u32[]{:S(2)}) copy-start(f32[2,54,216]{2,0,1:T(2,128)} %param.25) | copy-start | bytes 279940
  147.1 24.0 %copy-start.25 = (f32[2,54,216]{2,0,1:T(2,128)S(1)}, f32[2,54,216]{2,0,1:T(2,128)}, u32[]{:S(2)}) copy-start(f32[2,54,216]{2,0,1:T(2,128)} %param.26) | copy-start | bytes 279940
  147.2 21.8 %all-to-all-start.2 = ((bf16[8,138,216]{2,1,0:T(8,128)(2,1)}), bf16[8,138,216]{2,1,0:T(8,128)(2,1)S(1)}, u32[]{:S(2)}, u32[]{:S(2)}) async-start(bf16[8,138,216]{2,1,0:T(8,128)(2,1)} %pad_maximum_fusion), calls=%async_computation.2 | async-start | bytes 1179648 | tf_op jit(solution)/shard_map/all_to_all | solution.py:313
  159.5 14.5 %copy-start.50 = (f32[4,216]{1,0:T(4,128)S(1)}, f32[4,216]{1,0:T(4,128)}, u32[]{:S(2)}) copy-start(f32[4,216]{1,0:T(4,128)} %param.27) | copy-start | bytes 10372
  159.5 14.5 %copy-start.60 = (f32[4,216]{1,0:T(4,128)S(1)}, f32[4,216]{1,0:T(4,128)}, u32[]{:S(2)}) copy-start(f32[4,216]{1,0:T(4,128)} %param.28) | copy-start | bytes 10372
  159.5 14.5 %copy-start.61 = (f32[4,216]{1,0:T(4,128)S(1)}, f32[4,216]{1,0:T(4,128)}, u32[]{:S(2)}) copy-start(f32[4,216]{1,0:T(4,128)} %param.29) | copy-start | bytes 10372
  159.5 15.1 %copy-start.28 = (f32[9,216]{1,0:T(8,128)S(1)}, f32[9,216]{1,0:T(8,128)}, u32[]{:S(2)}) copy-start(f32[9,216]{1,0:T(8,128)} %param.33) | copy-start | bytes 23332
  159.5 15.1 %copy-start.48 = (f32[9,216]{1,0:T(8,128)S(1)}, f32[9,216]{1,0:T(8,128)}, u32[]{:S(2)}) copy-start(f32[9,216]{1,0:T(8,128)} %param.34) | copy-start | bytes 23332
  159.5 15.1 %copy-start.49 = (f32[9,216]{1,0:T(8,128)S(1)}, f32[9,216]{1,0:T(8,128)}, u32[]{:S(2)}) copy-start(f32[9,216]{1,0:T(8,128)} %param.35) | copy-start | bytes 23332
  (24 other events, 86.9 us)
where the time goes:
time: 177 us; the launch traced here: 175 us
  matrix products  44.6 us (25%)
  local copies, waits for them, and re-layouts  39.8 us (22%)
  blocking collectives  34.5 us (19%)
  other arithmetic  20.8 us (12%)
  starting transfers between devices  16.9 us (10%)
  waiting for transfers between devices  14.8 us (8%)
  between operations  3.87 us (2%)
    all_to_all x1, waiting for transfers between devices, local(): lax.all_to_all(message, 'head', split_axis=0, concat_axis=0, tiled=True)  14.2 us
    unnamed x159, local copies, waits for them, and re-layouts  10.6 us
    all_gather x1, blocking collectives, local(): ffn_blocks = lax.all_gather(blocks[4:12], 'head', axis=0)  9.25 us
    reduce_sum x1, other arithmetic, conv_back(): jnp.sum(grad_grid * shifted(padded_hidden, row_off, col_off), axis=(0, 1,...  7.31 us
    all_to_all x1, starting transfers between devices, gather_blocks(): lax.all_to_all(jnp.broadcast_to(mine[None], (data_devices,) + mine.shape)...  7.25 us
    all_gather x1, blocking collectives, local(): attn_blocks = lax.all_gather(blocks[0:4], 'head', axis=0)  6.93 us
    all_gather x1, blocking collectives, local(): lax.all_gather(my_token_grad.astype(jnp.bfloat16), 'head', axis=0, tiled=...  6.68 us
    all_gather x1, blocking collectives, local(): lax.all_gather(my_output.astype(jnp.bfloat16), 'head', axis=0, tiled=True)  6.18 us
  transfers between devices with their start and end apart: 3, of which 2 were waited for; matrix products, arithmetic and copies ran while one was open for 6% of the time, Pallas kernels for 0%

commit v1 on v0

--- a/solution.py
+++ b/solution.py
@@ -14,6 +14,22 @@
 decay_matrix = 0.05
 adam_steps = 3
 highest = lax.Precision.HIGHEST
+
+
+def gather_around(x, axis, dim):
+    ways, here, step = (lax.axis_size(axis), lax.axis_index(axis), x.shape[dim])
+    dims = [n * ways if d == dim else n for d, n in enumerate(x.shape)]
+    full = lax.dynamic_update_slice_in_dim(jnp.zeros(dims, x.dtype), x, here * step, axis=dim)
+    going_up = going_down = x
+    for far in range(1, ways // 2 + 1):
+        going_up = lax.ppermute(going_up, axis, [(d, (d + 1) % ways) for d in range(ways)])
+        full = lax.dynamic_update_slice_in_dim(full, going_up, (here - far) % ways * step, axis=dim)
+        if 2 * far < ways:
+            going_down = lax.ppermute(going_down, axis, [(d, (d - 1) % ways) for d in range(ways)])
+            full = lax.dynamic_update_slice_in_dim(
+                full, going_down, (here + far) % ways * step, axis=dim
+            )
+    return full
 
 
 def normalize(values, gain_row, bias_row):
@@ -265,9 +281,7 @@
     my_token_grad = grad_middle + normalize_back(
         grad_normed_one, scaled_one, inverse_one, norm_params[0]
     )
-    token_grad = lax.all_gather(
-        my_token_grad.astype(jnp.bfloat16), "head", axis=0, tiled=True
-    ).astype(jnp.float32)
+    token_grad = gather_around(my_token_grad.astype(jnp.bfloat16), "head", 0).astype(jnp.float32)
     norm_part = jnp.stack(
         [
             jnp.sum(grad_normed_one * scaled_one, axis=(0, 1)),

time: 177 us -> 195 us (1.10)
  local copies, waits for them, and re-layouts: 39.8 us -> 56.8 us
  waiting for transfers between devices: 14.8 us -> 20.9 us
  blocking collectives: 34.5 us -> 28.9 us
    dynamic_update_slice x0 -> x4, local copies, waits for them, and re-layouts: none -> 13.7 us  [the longest x2 6.74 us: gather_around(): lax.dynamic_update_slice_in_dim(full, going_up, (here - far) % ways * ste...]
    all_gather x1 -> x0, blocking collectives: 6.68 us -> none  [local(): lax.all_gather(my_token_grad.astype(jnp.bfloat16), 'head', axis=0, tiled=...]
    ppermute x0 -> x3, waiting for transfers between devices: none -> 3.6 us  [the longest x2 3.59 us: gather_around(): lax.ppermute(going_up, axis, [(d, (d + 1) % ways) for d in range(ways)])]
    another operation x10, local copies, waits for them, and re-layouts: 0.72 us -> 4.28 us  [conv_back(): return (grad_hidden.reshape(hidden.shape), jnp.stack(kernel_rows))]
    all_to_all x1, waiting for transfers between devices: 14.2 us -> 17.3 us  [local(): lax.all_to_all(message, 'head', split_axis=0, concat_axis=0, tiled=True)]
    convert_element_type x4, local copies, waits for them, and re-layouts: 2.94 us -> 0.72 us  [local(): by_head(m).astype(jnp.bfloat16)]
    unnamed x159 -> x166, local copies, waits for them, and re-layouts: 10.6 us -> 11.4 us
  transfers between devices with their start and end apart: 3 -> 6, of which waited for: 2 -> 2; matrix products, arithmetic and copies ran while one was open for 6% -> 12% of each run, Pallas kernels for 0% -> 0%
where the time goes in v1:
time: 195 us; the launch traced here: 194 us
  local copies, waits for them, and re-layouts  56.8 us (29%)
  matrix products  43.7 us (22%)
  blocking collectives  28.9 us (15%)
  other arithmetic  21.6 us (11%)
  waiting for transfers between devices  20.9 us (11%)
  starting transfers between devices  17.5 us (9%)
  between operations  4.15 us (2%)
    all_to_all x1, waiting for transfers between devices, local(): lax.all_to_all(message, 'head', split_axis=0, concat_axis=0, tiled=True)  17.3 us
    unnamed x166, local copies, waits for them, and re-layouts  11.4 us
    all_gather x1, blocking collectives, local(): ffn_blocks = lax.all_gather(blocks[4:12], 'head', axis=0)  9.25 us
    all_gather x1, blocking collectives, local(): lax.all_gather(my_output.astype(jnp.bfloat16), 'head', axis=0, tiled=True)  7.31 us
    all_to_all x1, starting transfers between devices, gather_blocks(): lax.all_to_all(jnp.broadcast_to(mine[None], (data_devices,) + mine.shape)...  7.25 us
    reduce_sum x1, other arithmetic, conv_back(): jnp.sum(grad_grid * shifted(padded_hidden, row_off, col_off), axis=(0, 1,...  7.16 us
    all_gather x1, blocking collectives, local(): attn_blocks = lax.all_gather(blocks[0:4], 'head', axis=0)  6.93 us
    dynamic_update_slice x2, local copies, waits for them, and re-layouts, gather_around(): lax.dynamic_update_slice_in_dim(full, going_up, (here - far) % ways * ste...  6.74 us
  transfers between devices with their start and end apart: 6, of which 2 were waited for; matrix products, arithmetic and copies ran while one was open for 12% of the time, Pallas kernels for 0%

profile of v1, /device:TPU:0, one launch (start us, length us, event | category | flops | bytes accessed | tf_op | source)
XLA Modules:
  0.0 193.6 jit_solution(17813068040309853297)
XLA Ops:
  0.7 1.0 convert_element_type.208
  1.7 1.0 broadcast_in_dim.23
  2.7 7.3 %all-to-all-start = ((bf16[8,2,54,216]{3,1,2,0:T(2,128)(2,1)}), bf16[8,2,54,216]{3,1,2,0:T(2,128)(2,1)S(1)}, u32[]{:S(2)}, u32[]{:S(2)}) async-start(bf16[8,2,54,216]{3,1,2,0:T(2,128)(2,1)} %broadcast_in_dim.23), calls=%async_computation | async-start | bytes 884736 | tf_op jit(solution)/shard_map/all_to_all | solution.py:121
  13.3 5.4 %all-gather.2 = f32[4,216,9]{1,2,0:T(8,128)S(1)} all-gather(f32[1,216,9]{1,2,0:T(8,128)} %bitcast.275), channel_id=1, replica_groups=mesh['dp'=8,'head'=4] {'head'}, dimensions={0}, use_global_device_ids=true | all-gather | bytes 38880 | tf_op jit(solution)/shard_map/all_gather | solution.py:179
  19.8 1.2 constant_dynamic-slice_fusion.1
  23.7 6.9 %all-gather = bf16[16,54,216]{2,1,0:T(8,128)(2,1)S(1)} all-gather(bf16[4,54,216]{2,1,0:T(8,128)(2,1)S(1)} %slice.225), channel_id=2, replica_groups=mesh['dp'=8,'head'=4] {'head'}, dimensions={0}, use_global_device_ids=true | all-gather | bytes 466560 | tf_op jit(solution)/shard_map/all_gather | solution.py:177
  34.0 9.3 %all-gather.1 = bf16[32,54,216]{2,0,1:T(8,128)(2,1)S(1)} all-gather(bf16[8,54,216]{2,0,1:T(8,128)(2,1)S(1)} %copy.298), channel_id=3, replica_groups=mesh['dp'=8,'head'=4] {'head'}, dimensions={0}, use_global_device_ids=true | all-gather | bytes 933120 | tf_op jit(solution)/shard_map/all_gather | solution.py:178
  43.7 1.0 reshape.508
  45.5 2.0 %bitcast_reduce_fusion = (f32[12,196]{0,1:T(8,128)S(1)}, f32[196,196,12]{1,2,0:T(8,128)S(1)}) fusion(f32[2,12,12]{2,1,0:T(8,128)S(1)} %copy.293, bf16[12,196,196]{2,1,0:T(8,128)(2,1)S(1)} %multiply_convert_fusion), kind=kOutput, calls=%fused_computation.15 | convolution fusion | flops 66841488 | bytes 3090368 | tf_op jit(solution)/shard_map/mn,gnqk->gmqk/dot_general | solution.py:84
  47.5 1.1 fusion.12
  49.3 3.9 %fusion.28 = bf16[12,196,196]{2,0,1:T(8,128)(2,1)S(1)} fusion(f32[2,12,12]{2,1,0:T(8,128)S(1)} %copy.293, f32[196,196,12]{1,2,0:T(8,128)S(1)} %get-tuple-element.163, f32[12,196]{0,1:T(8,128)S(1)} %fusion.12, f32[12,196]{0,1:T(8,128)S(1)} %get-tuple-element.162), kind=kOutput, calls=%fused_computation.30 | convolution fusion | flops 67765824 | bytes 4346240 | tf_op jit(solution)/shard_map/jm,gmqk->gjqk/dot_general | solution.py:88
  53.2 1.2 copy-done.3
  55.6 1.2 fusion.111
  56.8 1.2 reshape.507
  58.0 1.8 multiply_convert_fusion.1
  59.7 2.1 %reshape.510 = f32[196,864]{1,0:T(8,128)} reshape(f32[1,14,14,864]{3,2,1,0:T(8,128)} %get-tuple-element.144) | data formatting | bytes 1354752 | tf_op jit(solution)/shard_map/reshape | solution.py:64
  61.8 2.0 %fusion.81 = bf16[864,196]{0,1:T(8,128)(2,1)} fusion(f32[864]{0:T(1024)S(1)} %fusion.125, f32[196,864]{1,0:T(8,128)} %reshape.510), kind=kLoop, calls=%fused_computation.123 | loop fusion | flops 1016064 | bytes 1019520 | tf_op jit(solution)/shard_map/gsu,gsd->ud/dot_general | solution.py:227
  63.9 3.5 %multiply_reduce_fusion.8 = (f32[864]{0:T(1024)}, f32[196,864]{1,0:T(8,128)}) fusion(f32[196,864]{1,0:T(8,128)} %fusion.111, f32[196,864]{1,0:T(8,128)} %reshape.510, f32[864]{0:T(1024)S(1)} %fusion.125, bf16[864,216]{1,0:T(8,128)(2,1)} %reshape.508, f32[]{:T(128)} %bitcast.30, f32[1,196,216]{2,0,1:T(1,128)} %constant_dynamic-slice_fusion), kind=kOutput, calls=%fused_computation.116 | convolution fusion | flops 75103200 | bytes 2581636 | tf_op jit(solution)/shard_map/gsd,ud->gsu/dot_general | solution.py:229
  67.3 2.1 %reshape.511 = f32[1,14,14,864]{3,2,1,0:T(8,128)} reshape(f32[196,864]{1,0:T(8,128)} %get-tuple-element.171) | data formatting | bytes 1354752 | tf_op jit(solution)/shard_map/reshape | solution.py:52
  69.4 7.2 %multiply_reduce_fusion = (f32[864]{0:T(1024)}, f32[864]{0:T(1024)}, f32[864]{0:T(1024)}, f32[864]{0:T(1024)}, f32[864]{0:T(1024)}, /*index=5*/f32[864]{0:T(1024...) fusion(f32[1,14,14,864]{3,2,1,0:T(8,128)} %reshape.511, f32[1,14,14,864]{3,2,1,0:T(8,128)S(1)} %reshape.507, ...), kind=kLoop, calls=%fused_computation.106 | loop fusion | flops 5750784 | bytes 1752192 | tf_op jit(solution)/shard_map/reduce_sum | solution.py:78
  76.6 1.2 convert_element_type.227
  77.8 1.8 fusion.97
  79.6 1.3 fusion.136
  80.9 1.1 fusion.100
  82.0 1.1 fusion.36
  83.2 1.9 fusion.44
  85.6 3.4 %fusion.48 = f32[12,12]{1,0:T(8,128)} fusion(bf16[12,196,196]{2,1,0:T(8,128)(2,1)S(1)} %convolution_convert_fusion, f32[196,196,12]{1,2,0:T(8,128)S(1)} %copy-done.2, f32[12,196]{0,1:T(8,128)S(1)} %copy-done.28, f32[12,196]{0,1:T(8,128)S(1)} %copy-done.24), kind=kOutput, calls=%fused_computation.66 | convolution fusion | flops 67304832 | bytes 2785344 | tf_op jit(solution)/shard_map/gjqk,gmqk->jm/dot_general | solution.py:96
  89.0 4.1 %fusion.4 = (f32[12,196]{0,1:T(8,128)S(1)}, f32[196,196,12]{1,2,0:T(8,128)S(1)}) fusion(f32[12,196]{0,1:T(8,128)S(1)} %copy-done.28, f32[12,196]{0,1:T(8,128)S(1)} %copy-done.24, f32[196,196,12]{1,2,0:T(8,128)S(1)} %copy-done.2, f32[2,12,12]{2,1,0:T(8,128)S(1)} %copy.293, bf16[12,196,196]{2,1,0:T(8,128)(2,1)S(1)} %convolution_convert_fusion), kind=kOutput, calls=%fused_computation.8 | convolution fusion | flops 68224464 | bytes 6506432 | tf_op jit(solution)/shard_map/jm,gjqk->gmqk/dot_general | solution.py:95
  93.1 3.9 %fusion.53 = f32[12,12]{1,0:T(8,128)} fusion(bf16[12,196,196]{2,1,0:T(8,128)(2,1)S(1)} %multiply_convert_fusion, f32[12,196]{0,1:T(8,128)S(1)} %get-tuple-element.167, f32[196,196,12]{1,2,0:T(8,128)S(1)} %get-tuple-element.168, f32[196,196,12]{1,2,0:T(8,128)S(1)} %copy-done.2, f32[12,196]{0,1:T(8,128)S(1)} %copy-done.28, f32[12,196]{0,1:T(8,128)S(1)} %copy-done.24), kind=kOutput, calls=%fused_computation.67 | convolution fusion | flops 68226816 | bytes 4638720 | tf_op jit(solution)/shard_map/gmqk,gnqk->mn/dot_general | solution.py:98
  97.0 4.7 %fusion.25 = bf16[12,196,196]{2,0,1:T(8,128)(2,1)S(1)} fusion(f32[196,196,12]{1,2,0:T(8,128)S(1)} %get-tuple-element.168, f32[12,196]{0,1:T(8,128)S(1)} %get-tuple-element.167, f32[2,12,12]{2,1,0:T(8,128)S(1)} %copy.293, f32[196,196,12]{1,2,0:T(8,128)S(1)} %copy-done.2, f32[12,196]{0,1:T(8,128)S(1)} %copy-done.28, f32[12,196]{0,1:T(8,128)S(1)} %copy-done.24), kind=kOutput, calls=%fused_computation.29 | convolution fusion | flops 68687808 | bytes 7659904 | tf_op jit(solution)/shard_map/mn,gmqk->gnqk/dot_general | solution.py:101
  101.9 1.2 fusion.45
  103.0 1.1 fusion.46
  114.4 1.1 fusion.147
  115.5 1.1 convolution_add_fusion.1
  116.6 1.2 fusion.95
  123.7 3.7 %concatenate.19 = bf16[4,678,216]{1,2,0:T(8,128)(2,1)} concatenate(bf16[4,54,216]{1,2,0:T(8,128)(2,1)S(1)} %copy.317, bf16[4,54,216]{1,2,0:T(8,128)(2,1)S(1)} %copy.318, bf16[4,54,216]{1,2,0:T(8,128)(2,1)S(1)} %copy.319, bf16[4,54,216]{1,2,0:T(8,128)(2,1)S(1)} %copy.320, bf16[4,216,216]{1,2,0:T(8,128)(2,1)S(1)} %convolution_convert_fusion.2, ...), dimensions={1} | concatenate | bytes 2343168 | tf_op jit(solution)/shard_map/concatenate | solution.py:304
  127.4 3.7 %all-to-all-start.1 = ((bf16[4,678,216]{1,2,0:T(8,128)(2,1)}), bf16[4,678,216]{1,2,0:T(8,128)(2,1)S(1)}, u32[]{:S(2)}, u32[]{:S(2)}) async-start(bf16[4,678,216]{1,2,0:T(8,128)(2,1)} %concatenate.19), calls=%async_computation.1 | async-start | bytes 2654208 | tf_op jit(solution)/shard_map/all_to_all | solution.py:309
  131.2 17.3 %all-to-all-done.1 = bf16[4,678,216]{1,2,0:T(8,128)(2,1)S(1)} async-done(((bf16[4,678,216]{1,2,0:T(8,128)(2,1)}), bf16[4,678,216]{1,2,0:T(8,128)(2,1)S(1)}, u32[]{:S(2)}, u32[]{:S(2)}) %all-to-all-start.1) | async-done | bytes 1171616 | tf_op jit(solution)/shard_map/all_to_all | solution.py:309
  149.4 1.1 scatter_fusion
  151.6 6.0 %all-to-all-start.2 = ((bf16[8,138,216]{2,1,0:T(8,128)(2,1)}), bf16[8,138,216]{2,1,0:T(8,128)(2,1)S(1)}, u32[]{:S(2)}, u32[]{:S(2)}) async-start(bf16[8,138,216]{2,1,0:T(8,128)(2,1)} %pad_maximum_fusion), calls=%async_computation.2 | async-start | bytes 1179648 | tf_op jit(solution)/shard_map/all_to_all | solution.py:327
  159.0 3.6 %collective-permute-done = bf16[1,196,216]{2,1,0:T(8,128)(2,1)S(1)} collective-permute-done((bf16[1,196,216]{2,1,0:T(8,128)(2,1)S(1)}, bf16[1,196,216]{2,1,0:T(8,128)(2,1)S(1)}, u32[]{:S(2)}, u32[]{:S(2)}) %collective-permute-start) | collective-permute-done | bytes 84704 | tf_op jit(solution)/shard_map/ppermute | solution.py:25
  162.6 7.3 %all_gather.23 = bf16[4,196,216]{2,1,0:T(8,128)(2,1)S(1)} all-gather(bf16[1,196,216]{2,1,0:T(8,128)(2,1)S(1)} %fusion.43), channel_id=1, replica_groups=mesh['dp'=8,'head'=4] {'head'}, dimensions={0}, use_global_device_ids=true | all-gather | bytes 423360 | tf_op jit(solution)/shard_map/all_gather | solution.py:222
  170.0 1.0 copy.333
  171.2 3.6 %dynamic_update_slice.12 = bf16[4,196,216]{2,0,1:T(4,128)(2,1)S(1)} dynamic-update-slice(bf16[4,196,216]{2,0,1:T(4,128)(2,1)S(1)} %broadcast_in_dim.26, bf16[1,196,216]{2,0,1:T(2,128)(2,1)S(1)} %copy.308, s32[]{:T(128)S(6)} %select_n.39, s32[]{:T(128)} %constant.43.clone.1, s32[]{:T(128)} %constant.43.clone.1) | dynamic-update-slice | bytes 169348 | tf_op jit(solution)/shard_map/dynamic_update_slice | solution.py:22
  175.0 3.4 %dynamic_update_slice.13 = bf16[4,196,216]{2,0,1:T(4,128)(2,1)S(1)} dynamic-update-slice(bf16[4,196,216]{2,0,1:T(4,128)(2,1)S(1)} %dynamic_update_slice.12, bf16[1,196,216]{2,0,1:T(2,128)(2,1)S(1)} %copy.309, s32[]{:T(128)S(6)} %select_n.43, s32[]{:T(128)} %constant.43.clone.1, s32[]{:T(128)} %constant.43.clone.1) | dynamic-update-slice | bytes 169348 | tf_op jit(solution)/shard_map/dynamic_update_slice | solution.py:26
  178.4 1.1 copy.310
  179.4 3.4 %dynamic_update_slice.14 = bf16[4,196,216]{2,0,1:T(4,128)(2,1)S(1)} dynamic-update-slice(bf16[4,196,216]{2,0,1:T(4,128)(2,1)S(1)} %dynamic_update_slice.13, bf16[1,196,216]{2,0,1:T(2,128)(2,1)S(1)} %copy.310, s32[]{:T(128)S(6)} %select_n.45, s32[]{:T(128)} %constant.43.clone.1, s32[]{:T(128)} %constant.43.clone.1) | dynamic-update-slice | bytes 169348 | tf_op jit(solution)/shard_map/dynamic_update_slice | solution.py:29
  183.0 3.4 %dynamic_update_slice.15 = bf16[4,196,216]{2,0,1:T(4,128)(2,1)S(1)} dynamic-update-slice(bf16[4,196,216]{2,0,1:T(4,128)(2,1)S(1)} %dynamic_update_slice.14, bf16[1,196,216]{2,0,1:T(2,128)(2,1)S(1)} %copy.311, s32[]{:T(128)S(6)} %select_n.47, s32[]{:T(128)} %constant.43.clone.1, s32[]{:T(128)} %constant.43.clone.1) | dynamic-update-slice | bytes 169348 | tf_op jit(solution)/shard_map/dynamic_update_slice | solution.py:26
  (284 shorter events, 38.6 us)
Async XLA Ops:
  0.6 18.3 %copy-start = (f32[4,196,216]{2,0,1:T(4,128)S(1)}, f32[4,196,216]{2,0,1:T(4,128)}, u32[]{:S(2)}) copy-start(f32[4,196,216]{2,0,1:T(4,128)} %param.19) | copy-start | bytes 2032132
  2.7 20.2 %all-to-all-start = ((bf16[8,2,54,216]{3,1,2,0:T(2,128)(2,1)}), bf16[8,2,54,216]{3,1,2,0:T(2,128)(2,1)S(1)}, u32[]{:S(2)}, u32[]{:S(2)}) async-start(bf16[8,2,54,216]{3,1,2,0:T(2,128)(2,1)} %broadcast_in_dim.23), calls=%async_computation | async-start | bytes 884736 | tf_op jit(solution)/shard_map/all_to_all | solution.py:121
  11.9 41.3 %copy-start.71 = (f32[12]{0:T(128)}, f32[12]{0:T(128)S(1)}, u32[]{:S(2)}) copy-start(f32[12]{0:T(128)S(1)} %compare_convert_fusion) | copy-start | bytes 148
  21.1 33.8 %copy-start.4 = (bf16[1,196,216]{2,1,0:T(8,128)(2,1)}, bf16[1,196,216]{2,1,0:T(8,128)(2,1)S(1)}, u32[]{:S(2)}) copy-start(bf16[1,196,216]{2,1,0:T(8,128)(2,1)S(1)} %get-tuple-element.146) | copy-start | bytes 254020
  21.2 11.7 %copy-start.37 = (f32[196]{0:T(256)}, f32[196]{0:T(256)S(1)}, u32[]{:S(2)}) copy-start(f32[196]{0:T(256)S(1)} %broadcast_multiply_fusion.5) | copy-start | bytes 2356
  22.0 10.8 %copy-start.60 = (f32[196]{0:T(256)}, f32[196]{0:T(256)S(1)}, u32[]{:S(2)}) copy-start(f32[196]{0:T(256)S(1)} %add_rsqrt_fusion.1) | copy-start | bytes 2356
  22.9 10.0 %copy-start.40 = (f32[1,216]{1,0:T(1,128)}, f32[1,216]{1,0:T(1,128)S(1)}, u32[]{:S(2)}) copy-start(f32[1,216]{1,0:T(1,128)S(1)} %get-tuple-element.160) | copy-start | bytes 2596
  22.9 10.0 %copy-start.72 = (f32[1,216]{1,0:T(1,128)}, f32[1,216]{1,0:T(1,128)S(1)}, u32[]{:S(2)}) copy-start(f32[1,216]{1,0:T(1,128)S(1)} %get-tuple-element.159) | copy-start | bytes 2596
  22.9 32.6 %copy-start.33 = (f32[1,216]{1,0:T(1,128)}, f32[1,216]{1,0:T(1,128)S(1)}, u32[]{:S(2)}) copy-start(f32[1,216]{1,0:T(1,128)S(1)} %get-tuple-element.158) | copy-start | bytes 2596
  22.9 32.6 %copy-start.62 = (f32[1,216]{1,0:T(1,128)}, f32[1,216]{1,0:T(1,128)S(1)}, u32[]{:S(2)}) copy-start(f32[1,216]{1,0:T(1,128)S(1)} %get-tuple-element.161) | copy-start | bytes 2596
  32.3 12.6 %copy-start.10 = (bf16[196,12,18]{0,2,1:T(8,128)(2,1)}, bf16[196,12,18]{0,2,1:T(8,128)(2,1)S(1)}, u32[]{:S(2)}) copy-start(bf16[196,12,18]{0,2,1:T(8,128)(2,1)S(1)} %reshape.501) | copy-start | bytes 254020
  32.4 11.1 %copy-start.21 = (bf16[216,216]{1,0:T(8,128)(2,1)}, bf16[216,216]{1,0:T(8,128)(2,1)S(1)}, u32[]{:S(2)}) copy-start(bf16[216,216]{1,0:T(8,128)(2,1)S(1)} %reshape_squeeze.13) | copy-start | bytes 279940
  32.8 12.2 %copy-start.12 = (bf16[196,12,18]{0,2,1:T(8,128)(2,1)}, bf16[196,12,18]{0,2,1:T(8,128)(2,1)S(1)}, u32[]{:S(2)}) copy-start(bf16[196,12,18]{0,2,1:T(8,128)(2,1)S(1)} %reshape.500) | copy-start | bytes 254020
  34.0 19.3 %copy-start.14 = (bf16[196,12,18]{0,2,1:T(8,128)(2,1)}, bf16[196,12,18]{0,2,1:T(8,128)(2,1)S(1)}, u32[]{:S(2)}) copy-start(bf16[196,12,18]{0,2,1:T(8,128)(2,1)S(1)} %reshape.499) | copy-start | bytes 254020
  76.6 8.5 %copy-start.15 = (bf16[196,12,18]{0,2,1:T(8,128)(2,1)S(1)}, bf16[196,12,18]{0,2,1:T(8,128)(2,1)}, u32[]{:S(2)}) copy-start(bf16[196,12,18]{0,2,1:T(8,128)(2,1)} %copy-done.14) | copy-start | bytes 254020
  76.6 9.0 %copy-start.24 = (f32[12,196]{0,1:T(8,128)S(1)}, f32[12,196]{0,1:T(8,128)}, u32[]{:S(2)}) copy-start(f32[12,196]{0,1:T(8,128)} %copy-done.23) | copy-start | bytes 28228
  76.6 9.0 %copy-start.28 = (f32[12,196]{0,1:T(8,128)S(1)}, f32[12,196]{0,1:T(8,128)}, u32[]{:S(2)}) copy-start(f32[12,196]{0,1:T(8,128)} %copy-done.27) | copy-start | bytes 28228
  101.8 8.0 %copy-start.32 = (f32[196]{0:T(256)S(1)}, f32[196]{0:T(256)}, u32[]{:S(2)}) copy-start(f32[196]{0:T(256)} %copy-done.31) | copy-start | bytes 2356
  105.6 11.0 %copy-start.41 = (f32[1,216]{1,0:T(1,128)S(1)}, f32[1,216]{1,0:T(1,128)}, u32[]{:S(2)}) copy-start(f32[1,216]{1,0:T(1,128)} %copy-done.40) | copy-start | bytes 2596
  110.3 11.5 %copy-start.57 = (f32[1,4,216]{2,1,0:T(4,128)S(1)}, f32[1,4,216]{2,1,0:T(4,128)}, u32[]{:S(2)}) copy-start(f32[1,4,216]{2,1,0:T(4,128)} %stack.61) | copy-start | bytes 10372
  110.3 11.5 %copy-start.54 = (f32[1,4,216]{2,1,0:T(4,128)S(1)}, f32[1,4,216]{2,1,0:T(4,128)}, u32[]{:S(2)}) copy-start(f32[1,4,216]{2,1,0:T(4,128)} %stack.62) | copy-start | bytes 10372
  110.3 11.5 %copy-start.56 = (f32[1,4,216]{2,1,0:T(4,128)S(1)}, f32[1,4,216]{2,1,0:T(4,128)}, u32[]{:S(2)}) copy-start(f32[1,4,216]{2,1,0:T(4,128)} %stack.63) | copy-start | bytes 10372
  110.4 11.5 %copy-start.55 = (f32[1,4,216]{2,1,0:T(4,128)S(1)}, f32[1,4,216]{2,1,0:T(4,128)}, u32[]{:S(2)}) copy-start(f32[1,4,216]{2,1,0:T(4,128)} %stack.64) | copy-start | bytes 10372
  110.5 11.4 %copy-start.64 = (f32[216]{0:T(256)S(1)}, f32[216]{0:T(256)}, u32[]{:S(2)}) copy-start(f32[216]{0:T(256)} %get-tuple-element.117) | copy-start | bytes 2596
  110.6 11.4 %copy-start.68 = (f32[216]{0:T(256)S(1)}, f32[216]{0:T(256)}, u32[]{:S(2)}) copy-start(f32[216]{0:T(256)} %get-tuple-element.113) | copy-start | bytes 2596
  127.4 22.0 %copy-start.70 = (s32[12]{0:T(128)S(1)}, s32[12]{0:T(128)}, u32[]{:S(2)}) copy-start(s32[12]{0:T(128)} %copy-done.69) | copy-start | bytes 148
  127.4 21.1 %all-to-all-start.1 = ((bf16[4,678,216]{1,2,0:T(8,128)(2,1)}), bf16[4,678,216]{1,2,0:T(8,128)(2,1)S(1)}, u32[]{:S(2)}, u32[]{:S(2)}) async-start(bf16[4,678,216]{1,2,0:T(8,128)(2,1)} %concatenate.19), calls=%async_computation.1 | async-start | bytes 2654208 | tf_op jit(solution)/shard_map/all_to_all | solution.py:309
  149.0 8.6 %copy-start.39 = (f32[196]{0:T(256)S(1)}, f32[196]{0:T(256)}, u32[]{:S(2)}) copy-start(f32[196]{0:T(256)} %copy-done.37) | copy-start | bytes 2356
  149.0 8.6 %copy-start.42 = (f32[1,216]{1,0:T(1,128)S(1)}, f32[1,216]{1,0:T(1,128)}, u32[]{:S(2)}) copy-start(f32[1,216]{1,0:T(1,128)} %copy-done.40) | copy-start | bytes 2596
  149.0 8.6 %copy-start.61 = (f32[196]{0:T(256)S(1)}, f32[196]{0:T(256)}, u32[]{:S(2)}) copy-start(f32[196]{0:T(256)} %copy-done.60) | copy-start | bytes 2356
  149.2 9.2 %copy-start.8 = (bf16[1,14,14,864]{3,2,1,0:T(8,128)(2,1)S(1)}, bf16[1,14,14,864]{3,2,1,0:T(8,128)(2,1)}, u32[]{:S(2)}) copy-start(bf16[1,14,14,864]{3,2,1,0:T(8,128)(2,1)} %get-tuple-element.143) | copy-start | bytes 1016068
  149.3 9.2 %copy-start.7 = (bf16[864,216]{1,0:T(8,128)(2,1)S(1)}, bf16[864,216]{1,0:T(8,128)(2,1)}, u32[]{:S(2)}) copy-start(bf16[864,216]{1,0:T(8,128)(2,1)} %reshape.508) | copy-start | bytes 1119748
  151.6 35.7 %all-to-all-start.2 = ((bf16[8,138,216]{2,1,0:T(8,128)(2,1)}), bf16[8,138,216]{2,1,0:T(8,128)(2,1)S(1)}, u32[]{:S(2)}, u32[]{:S(2)}) async-start(bf16[8,138,216]{2,1,0:T(8,128)(2,1)} %pad_maximum_fusion), calls=%async_computation.2 | async-start | bytes 1179648 | tf_op jit(solution)/shard_map/all_to_all | solution.py:327
  157.8 20.5 %collective-permute-start.1 = (bf16[1,196,216]{2,1,0:T(8,128)(2,1)S(1)}, bf16[1,196,216]{2,1,0:T(8,128)(2,1)}, u32[]{:S(2)}, u32[]{:S(2)}) collective-permute-start(bf16[1,196,216]{2,1,0:T(8,128)(2,1)S(1)} %fusion.94), channel_id=1, source_target_pairs={{0,3},{1,0},{2,1},{3,2},{4,7},{5,4},{6,5},{7,6},{8,11},{9,8},{10,9... | collective-permute-start | bytes 254024 | tf_op jit(solution)/shard_map/ppermute | solution.py:28
  157.9 4.7 %collective-permute-start = (bf16[1,196,216]{2,1,0:T(8,128)(2,1)S(1)}, bf16[1,196,216]{2,1,0:T(8,128)(2,1)S(1)}, u32[]{:S(2)}, u32[]{:S(2)}) collective-permute-start(bf16[1,196,216]{2,1,0:T(8,128)(2,1)S(1)} %fusion.94), channel_id=1, source_target_pairs={{0,1},{1,2},{2,3},{3,0},{4,5},{5,6},{6,7},{7,4},{8,9},{9,10},{10,1... | collective-permute-start | bytes 254024 | tf_op jit(solution)/shard_map/ppermute | solution.py:25
  162.6 20.2 %collective-permute-start.2 = (bf16[1,196,216]{2,1,0:T(8,128)(2,1)S(1)}, bf16[1,196,216]{2,1,0:T(8,128)(2,1)S(1)}, u32[]{:S(2)}, u32[]{:S(2)}) collective-permute-start(bf16[1,196,216]{2,1,0:T(8,128)(2,1)S(1)} %collective-permute-done), channel_id=1, source_target_pairs={{0,1},{1,2},{2,3},{3,0},{4,5},{5,6},{6,7},{7,4},{8,9},{9,10},{10,1... | collective-permute-start | bytes 254024 | tf_op jit(solution)/shard_map/ppermute | solution.py:25
  169.9 17.7 %copy-start.30 = (f32[2,12,12]{2,0,1:T(2,128)S(1)}, f32[2,12,12]{2,0,1:T(2,128)}, u32[]{:S(2)}) copy-start(f32[2,12,12]{2,0,1:T(2,128)} %param.30) | copy-start | bytes 3460
  169.9 17.7 %copy-start.58 = (f32[2,12,12]{2,0,1:T(2,128)S(1)}, f32[2,12,12]{2,0,1:T(2,128)}, u32[]{:S(2)}) copy-start(f32[2,12,12]{2,0,1:T(2,128)} %param.31) | copy-start | bytes 3460
  169.9 17.7 %copy-start.59 = (f32[2,12,12]{2,0,1:T(2,128)S(1)}, f32[2,12,12]{2,0,1:T(2,128)}, u32[]{:S(2)}) copy-start(f32[2,12,12]{2,0,1:T(2,128)} %param.32) | copy-start | bytes 3460
  169.9 19.5 %copy-start.20 = (f32[2,54,216]{2,0,1:T(2,128)S(1)}, f32[2,54,216]{2,0,1:T(2,128)}, u32[]{:S(2)}) copy-start(f32[2,54,216]{2,0,1:T(2,128)} %param.24) | copy-start | bytes 279940
  169.9 19.5 %copy-start.25 = (f32[2,54,216]{2,0,1:T(2,128)S(1)}, f32[2,54,216]{2,0,1:T(2,128)}, u32[]{:S(2)}) copy-start(f32[2,54,216]{2,0,1:T(2,128)} %param.25) | copy-start | bytes 279940
  170.0 19.5 %copy-start.26 = (f32[2,54,216]{2,0,1:T(2,128)S(1)}, f32[2,54,216]{2,0,1:T(2,128)}, u32[]{:S(2)}) copy-start(f32[2,54,216]{2,0,1:T(2,128)} %param.26) | copy-start | bytes 279940
  171.1 21.2 %copy-start.53 = (f32[4,216]{1,0:T(4,128)S(1)}, f32[4,216]{1,0:T(4,128)}, u32[]{:S(2)}) copy-start(f32[4,216]{1,0:T(4,128)} %param.27) | copy-start | bytes 10372
  171.1 21.2 %copy-start.65 = (f32[4,216]{1,0:T(4,128)S(1)}, f32[4,216]{1,0:T(4,128)}, u32[]{:S(2)}) copy-start(f32[4,216]{1,0:T(4,128)} %param.28) | copy-start | bytes 10372
  171.1 21.2 %copy-start.66 = (f32[4,216]{1,0:T(4,128)S(1)}, f32[4,216]{1,0:T(4,128)}, u32[]{:S(2)}) copy-start(f32[4,216]{1,0:T(4,128)} %param.29) | copy-start | bytes 10372
  171.2 21.8 %copy-start.29 = (f32[9,216]{1,0:T(8,128)S(1)}, f32[9,216]{1,0:T(8,128)}, u32[]{:S(2)}) copy-start(f32[9,216]{1,0:T(8,128)} %param.33) | copy-start | bytes 23332
  171.2 21.8 %copy-start.51 = (f32[9,216]{1,0:T(8,128)S(1)}, f32[9,216]{1,0:T(8,128)}, u32[]{:S(2)}) copy-start(f32[9,216]{1,0:T(8,128)} %param.34) | copy-start | bytes 23332
  171.2 21.8 %copy-start.52 = (f32[9,216]{1,0:T(8,128)S(1)}, f32[9,216]{1,0:T(8,128)}, u32[]{:S(2)}) copy-start(f32[9,216]{1,0:T(8,128)} %param.35) | copy-start | bytes 23332
  (31 other events, 152.8 us)
